TPU v7x, 32 devices: a whole 2x2x4 slice. The times are simulated.
32 devices in a mesh: facet: 4 (over y, x), band: 4 (over z), sub: 2 (over core).
Axes of the slice: x: 2, y: 2, z: 4, core: 2. Of those that a mesh axis runs over, the one named last changes fastest.
Arguments:
- facets: bfloat16 [8192, 2048], P(('facet', 'band')), may hold values from -6 to 6
- window: float32 [2048], replicated, may hold values from 0.5 to 1.5
- facet_offsets: int32 [4, 2], replicated, may hold values from 0 to 49151
- row_offsets: int32 [8], replicated, may hold values from 0 to 49151
- column_offset: int32 [1], replicated, may hold values from 0 to 49151
- kernel: bfloat16 [256, 256], replicated, may hold values from -0.375 to 0.375
- tile_counts: int32 [8, 16, 16], replicated, may hold values from 0 to 32
Outputs:
- residual: bfloat16 [8192, 2048], P(('facet', 'band'))
All inputs are finite; a program needn't handle non-finite values.
Results may differ from a plain program's by a relative error of at most 0.013.
Values may be sent and summed in bfloat16 or wider, within the bound.
A program may use at most 64 MiB of HBM per device.

v0:
```python
import math

import jax
import jax.numpy as jnp
from jax import lax
from jax.sharding import PartitionSpec as P

IMAGE = 49152


def modular_product(first, second):
    upper_bits = first // 256
    lower_bits = first % 256
    reduced = upper_bits * second % IMAGE
    reduced = reduced * 256 % IMAGE
    return (reduced + lower_bits * second) % IMAGE


def phase_table(frequency, position):
    reduced = modular_product(frequency % IMAGE, position % IMAGE)
    angle = reduced.astype(jnp.float32) * (2.0 * math.pi / IMAGE)
    return (jnp.cos(angle), jnp.sin(angle))


def product(left, right):
    return jnp.dot(left, right, preferred_element_type=jnp.float32)


def body(facets, window, facet_offsets, row_offsets, column_offset, kernel, tile_counts):
    facet_count = lax.axis_size("facet")
    band_count = lax.axis_size("band")
    sub_count = lax.axis_size("sub")
    facet_at = lax.axis_index("facet")
    band_at = lax.axis_index("band")
    sub_at = lax.axis_index("sub")
    band_rows = facets.shape[0]
    width = facets.shape[1]
    contrib = kernel.shape[0]
    sub_rows = contrib // band_count
    stacked = band_count * contrib
    a_scale = 1.0 / math.sqrt(width * facet_count)
    b_scale = 1.0 / math.sqrt(width)
    back_scale = 1.0 / math.sqrt(band_count * sub_count * contrib)
    out_scale = 1.0 / math.sqrt(contrib)
    offset = lax.dynamic_slice_in_dim(facet_offsets, facet_at, 1, 0)[0]
    cells = jnp.arange(width, dtype=jnp.int32)
    frequencies = jnp.arange(contrib, dtype=jnp.int32)
    cosine, sine = phase_table(column_offset[0] + frequencies[:, None], offset[1] + cells[None, :])
    col_real = (cosine * window[None, :] * b_scale).astype(jnp.bfloat16)
    col_imag = (-sine * window[None, :] * b_scale).astype(jnp.bfloat16)
    t_real = jnp.einsum("xy,ky->xk", facets, col_real, preferred_element_type=jnp.float32).astype(
        jnp.bfloat16
    )
    t_imag = jnp.einsum("xy,ky->xk", facets, col_imag, preferred_element_type=jnp.float32).astype(
        jnp.bfloat16
    )
    starts = lax.dynamic_slice_in_dim(row_offsets, sub_at * band_count, band_count, 0)
    row_freqs = (starts[:, None] + frequencies[None, :]).reshape(stacked)
    positions = offset[0] + band_at * band_rows + jnp.arange(band_rows, dtype=jnp.int32)
    row_cos, row_sin = phase_table(row_freqs[:, None], positions[None, :])
    a_real = (row_cos * a_scale).astype(jnp.bfloat16)
    a_imag = (-row_sin * a_scale).astype(jnp.bfloat16)
    part_real = product(a_real, t_real) - product(a_imag, t_imag)
    part_imag = product(a_real, t_imag) + product(a_imag, t_real)
    terms = jnp.stack([part_real, part_imag]).reshape(2, band_count, band_count, sub_rows, contrib)
    blocks = lax.psum_scatter(
        terms.astype(jnp.bfloat16), "band", scatter_dimension=2, tiled=True
    ).astype(jnp.float32)
    blocks = lax.psum(blocks, "facet")
    grid_part = blocks.reshape(2, band_count, sub_rows, contrib).astype(jnp.bfloat16)
    tiles = tile_counts.shape[1]
    tile_side = contrib // tiles
    counts = lax.dynamic_slice_in_dim(tile_counts, sub_at * band_count, band_count, 0).astype(
        jnp.float32
    )
    ratio = counts / (counts + 4.0)
    weights = jnp.broadcast_to(
        ratio[:, :, None, :, None], (band_count, tiles, tile_side, tiles, tile_side)
    )
    weights = weights.reshape(band_count, contrib, contrib)
    y_cols = jnp.einsum(
        "ij,cgrj->cgir", kernel, grid_part, preferred_element_type=jnp.float32
    ).astype(jnp.bfloat16)
    y_cols = lax.all_to_all(y_cols, "band", split_axis=2, concat_axis=3, tiled=True)
    z_cols = jnp.einsum("cgqi,ji->cgqj", y_cols, kernel, preferred_element_type=jnp.float32)
    weight_cols = jnp.swapaxes(
        lax.dynamic_slice_in_dim(weights, band_at * sub_rows, sub_rows, 2), 1, 2
    )
    w_cols = (weight_cols[None] * z_cols).astype(jnp.bfloat16)
    u_cols = jnp.einsum("cgqj,jl->cgql", w_cols, kernel, preferred_element_type=jnp.float32).astype(
        jnp.bfloat16
    )
    u_back = lax.all_to_all(u_cols, "band", split_axis=3, concat_axis=2, tiled=True)
    residual_grid = jnp.einsum(
        "cgqr,qm->cgrm", u_back, kernel, preferred_element_type=jnp.float32
    ).astype(jnp.bfloat16)
    back_real = (row_cos * back_scale).astype(jnp.bfloat16).reshape(band_count, contrib, band_rows)
    back_imag = (row_sin * back_scale).astype(jnp.bfloat16).reshape(band_count, contrib, band_rows)
    piece = lax.all_gather(residual_grid, "band", axis=2, tiled=True)
    e_real = jnp.einsum("gkx,gkl->xl", back_real, piece[0], preferred_element_type=jnp.float32)
    e_real = e_real - jnp.einsum(
        "gkx,gkl->xl", back_imag, piece[1], preferred_element_type=jnp.float32
    )
    e_imag = jnp.einsum("gkx,gkl->xl", back_real, piece[1], preferred_element_type=jnp.float32)
    e_imag = e_imag + jnp.einsum(
        "gkx,gkl->xl", back_imag, piece[0], preferred_element_type=jnp.float32
    )
    e_real, e_imag = (e_real, e_imag)
    e_real, e_imag = (
        lax.psum(e_real.astype(jnp.bfloat16), "sub").astype(jnp.float32),
        lax.psum(e_imag.astype(jnp.bfloat16), "sub").astype(jnp.float32),
    )
    out_cos = (cosine * out_scale).astype(jnp.bfloat16)
    out_sin = (sine * out_scale).astype(jnp.bfloat16)
    image = product(e_real.astype(jnp.bfloat16), out_cos) - product(
        e_imag.astype(jnp.bfloat16), out_sin
    )
    return (window[None, :] * image).astype(jnp.bfloat16)


def solution(mesh):
    in_specs = (P(("facet", "band"), None), P(), P(), P(), P(), P(), P())
    out_specs = P(("facet", "band"), None)
    return jax.shard_map(body, mesh=mesh, in_specs=in_specs, out_specs=out_specs, check_vma=False)
```

profile of v0, /device:TPU:1, one launch (start us, length us, event | category | flops | bytes accessed | tf_op | source)
XLA Modules:
  0.0 310.7 jit_solution(18280598410825204298)
XLA Ops:
  7.3 0.8 constant_dynamic-slice_fusion
  8.1 0.5 fusion.138
  8.7 0.7 add_select_fusion.9
  9.3 12.5 %convolution_convert_fusion.3 = bf16[256,512]{1,0:T(8,128)(2,1)} fusion(bf16[512,2048]{1,0:T(8,128)(2,1)S(1)} %copy-done, f32[2048]{0:T(1024)} %param.8, s32[256]{0:T(256)S(1)} %get-tuple-element.14, s32[2048]{0:T(1024)S(1)} %add_select_fusion.9, s32[256]{0:T(256)S(1)} %get-tuple-element.15), kind=kOutput, calls=%fused_computation.73 | convolution fusion | flops 551682048 | bytes 2377728 | tf_op jit(solution)/shard_map/xy,ky->xk/dot_general | solution.py:54
  21.9 10.5 %convolution_convert_fusion.4 = bf16[256,512]{1,0:T(8,128)(2,1)S(1)} fusion(bf16[512,2048]{1,0:T(8,128)(2,1)S(1)} %copy-done, f32[2048]{0:T(1024)S(1)} %copy-done.11, s32[256]{0:T(256)S(1)} %get-tuple-element.14, s32[2048]{0:T(1024)S(1)} %add_select_fusion.9, s32[256]{0:T(256)S(1)} %get-tuple-element.15), kind=kOutput, calls=%fused_computation.74 | convolution fusion | flops 551157760 | bytes 2377728 | tf_op jit(solution)/shard_map/xy,ky->xk/dot_general | solution.py:51
  33.2 10.7 %fusion.58 = f32[1024,256]{1,0:T(8,128)S(1)} fusion(bf16[256,512]{1,0:T(8,128)(2,1)S(1)} %convolution_convert_fusion.4, s32[1024]{0:T(1024)S(1)} %get-tuple-element.8, s32[512]{0:T(512)S(1)} %add_select_fusion.16, s32[1024]{0:T(1024)S(1)} %get-tuple-element.7), kind=kOutput, calls=%fused_computation.88 | convolution fusion | flops 282066944 | bytes 1320960 | tf_op jit(solution)/shard_map/dot_general | solution.py:26
  43.9 10.9 %fusion.57 = f32[1024,256]{1,0:T(8,128)S(1)} fusion(bf16[256,512]{1,0:T(8,128)(2,1)S(1)} %copy-done.14, s32[1024]{0:T(1024)S(1)} %get-tuple-element.8, s32[512]{0:T(512)S(1)} %add_select_fusion.16, s32[1024]{0:T(1024)S(1)} %get-tuple-element.7), kind=kOutput, calls=%fused_computation.87 | convolution fusion | flops 282066944 | bytes 1320960 | tf_op jit(solution)/shard_map/dot_general | solution.py:26
  54.8 11.6 %fusion.36 = bf16[1024,256]{1,0:T(8,128)(2,1)S(1)} fusion(f32[1024,256]{1,0:T(8,128)S(1)} %fusion.58, bf16[256,512]{1,0:T(8,128)(2,1)S(1)} %copy-done.14, s32[1024]{0:T(1024)S(1)} %get-tuple-element.8, s32[512]{0:T(512)S(1)} %add_select_fusion.16, s32[1024]{0:T(1024)S(1)} %get-tuple-element.7), kind=kOutput, calls=%fused_computation.59 | convolution fusion | flops 283115520 | bytes 1845248 | tf_op jit(solution)/shard_map/dot_general | solution.py:26
  66.4 11.8 %fusion.37 = bf16[1024,256]{1,0:T(8,128)(2,1)S(1)} fusion(f32[1024,256]{1,0:T(8,128)S(1)} %fusion.57, bf16[256,512]{1,0:T(8,128)(2,1)S(1)} %convolution_convert_fusion.4, s32[1024]{0:T(1024)S(1)} %get-tuple-element.8, s32[512]{0:T(512)S(1)} %add_select_fusion.16, s32[1024]{0:T(1024)S(1)} %get-tuple-element.7), kind=kOutput, calls=%fused_computation.60 | convolution fusion | flops 283115520 | bytes 1845248 | tf_op jit(solution)/shard_map/dot_general | solution.py:26
  78.3 1.0 copy.25
  79.4 29.1 %reduce-scatter.2.cloned.1.call-done = bf16[2,4,1,64,256]{4,3,1,0,2:T(8,128)(2,1)} async-done(((bf16[2,4,4,64,256]{4,3,1,0,2:T(8,128)(2,1)}), bf16[2,4,1,64,256]{4,3,1,0,2:T(8,128)(2,1)}) %reduce-scatter.2.cloned.1.call-update) | async-done | bytes 262160 | tf_op jit(solution)/shard_map/reduce_scatter | solution.py:66
  108.5 44.4 %all-reduce.4.cloned.1.call-done = bf16[2,4,1,64,256]{4,3,1,0,2:T(8,128)(2,1)} async-done(((bf16[2,4,1,64,256]{4,3,1,0,2:T(8,128)(2,1)}), bf16[2,4,1,64,256]{4,3,1,0,2:T(8,128)(2,1)}) %all-reduce.4.cloned.1.call-update) | async-done | bytes 262160 | tf_op jit(solution)/shard_map/psum | solution.py:69
  152.9 1.2 fusion.43
  154.4 1.1 reshape.290
  155.5 4.3 %all-to-all-start = ((bf16[4,2,16384]{2,1,0:T(2,128)(2,1)}), bf16[4,2,16384]{2,1,0:T(2,128)(2,1)S(1)}, u32[]{:S(2)}, u32[]{:S(2)}) async-start(bf16[4,2,16384]{2,1,0:T(2,128)(2,1)} %reshape.290), calls=%async_computation.1 | async-start | bytes 524288 | tf_op jit(solution)/shard_map/all_to_all | solution.py:84
  160.0 3.9 %broadcast_in_dim.2 = f32[4,16,16,16,16]{2,1,4,3,0:T(8,128)} broadcast(f32[4,16,16]{1,2,0:T(8,128)S(1)} %copy.17), dimensions={0,1,3} | broadcast | bytes 1052672 | tf_op jit(solution)/shard_map/broadcast_in_dim | solution.py:77
  163.8 6.1 %reshape.284 = f32[4,256,256]{1,2,0:T(8,128)S(1)} reshape(f32[4,16,16,16,16]{2,1,4,3,0:T(8,128)} %broadcast_in_dim.2) | data formatting | bytes 2097152 | tf_op jit(solution)/shard_map/reshape | solution.py:80
  169.9 0.7 dynamic-slice_bitcast_fusion
  171.0 0.4 copy.30
  171.8 1.4 convolution_convert_fusion.1
  173.5 0.4 reshape.292
  173.9 10.3 %all_to_all.36 = bf16[4,2,16384]{2,1,0:T(2,128)(2,1)S(1)} all-to-all(bf16[4,2,16384]{2,1,0:T(2,128)(2,1)S(1)} %reshape.292), channel_id=1, replica_groups=mesh['facet'=4,'band'=4,'sub'=2] {'band'}, dimensions={0} | all-to-all | bytes 524288 | tf_op jit(solution)/shard_map/all_to_all | solution.py:93
  184.6 0.4 copy.29
  185.3 0.9 convolution_convert_fusion
  186.5 28.7 %all-gather.2.cloned.1.call-done = bf16[2,4,256,256]{3,2,1,0:T(8,128)(2,1)} async-done(((bf16[2,4,64,256]{3,2,1,0:T(8,128)(2,1)}), bf16[2,4,256,256]{3,2,1,0:T(8,128)(2,1)}) %all-gather.2.cloned.1.call-update) | async-done | bytes 1048592 | tf_op jit(solution)/shard_map/all_gather | solution.py:99
  215.2 11.7 %convolution_bitcast_fusion = f32[512,256]{1,0:T(8,128)S(1)} fusion(s32[4,256]{1,0:T(4,128)S(1)} %get-tuple-element.12, s32[512]{0:T(512)S(1)} %copy-done.4, s32[4,256]{1,0:T(4,128)S(1)} %get-tuple-element.13, bf16[2,4,256,256]{3,2,1,0:T(8,128)(2,1)} %all-gather.2.cloned.1.call-done), kind=kOutput, calls=%fused_computation.61 | convolution fusion | flops 282066944 | bytes 1058816 | tf_op jit(solution)/shard_map/gkx,gkl->xl/dot_general | solution.py:105
  226.9 10.9 %convolution_bitcast_fusion.2 = f32[512,256]{1,0:T(8,128)S(1)} fusion(s32[4,256]{1,0:T(4,128)S(1)} %get-tuple-element.12, s32[512]{0:T(512)S(1)} %copy-done.4, s32[4,256]{1,0:T(4,128)S(1)} %get-tuple-element.13, bf16[2,4,256,256]{3,2,1,0:T(8,128)(2,1)S(1)} %copy-done.9), kind=kOutput, calls=%fused_computation.63 | convolution fusion | flops 282066944 | bytes 1058816 | tf_op jit(solution)/shard_map/gkx,gkl->xl/dot_general | solution.py:101
  237.9 11.3 %fusion.40 = bf16[512,256]{1,0:T(8,128)(2,1)} fusion(f32[512,256]{1,0:T(8,128)S(1)} %convolution_bitcast_fusion, s32[4,256]{1,0:T(4,128)S(1)} %get-tuple-element.12, s32[512]{0:T(512)S(1)} %copy-done.4, s32[4,256]{1,0:T(4,128)S(1)} %get-tuple-element.13, bf16[2,4,256,256]{3,2,1,0:T(8,128)(2,1)S(1)} %copy-done.9), kind=kOutput, calls=%fused_computation.68 | convolution fusion | flops 282329088 | bytes 1320960 | tf_op jit(solution)/shard_map/gkx,gkl->xl/dot_general | solution.py:104
  249.2 11.4 %fusion.41 = bf16[512,256]{1,0:T(8,128)(2,1)} fusion(f32[512,256]{1,0:T(8,128)S(1)} %convolution_bitcast_fusion.2, s32[4,256]{1,0:T(4,128)S(1)} %get-tuple-element.12, s32[512]{0:T(512)S(1)} %copy-done.4, s32[4,256]{1,0:T(4,128)S(1)} %get-tuple-element.13, bf16[2,4,256,256]{3,2,1,0:T(8,128)(2,1)S(1)} %copy-done.9), kind=kOutput, calls=%fused_computation.69 | convolution fusion | flops 282329088 | bytes 1320960 | tf_op jit(solution)/shard_map/gkx,gkl->xl/dot_general | solution.py:100
  260.6 19.1 %all-reduce.6.cloned.1.call-done = (bf16[512,256]{1,0:T(8,128)(2,1)}, bf16[512,256]{1,0:T(8,128)(2,1)}) async-done(((bf16[512,256]{1,0:T(8,128)(2,1)}, bf16[512,256]{1,0:T(8,128)(2,1)}), (bf16[512,256]{1,0:T(8,128)(2,1)}, bf16[512,256]{1,0:T(8,128)(2,1)})) %all-reduce.6.cloned.1.call-update) | async-done | bytes 524304 | tf_op jit(solution)/shard_map/psum | solution.py:110
  279.7 11.9 %fusion.44 = f32[512,2048]{1,0:T(8,128)S(1)} fusion(bf16[512,256]{1,0:T(8,128)(2,1)} %get-tuple-element.5, s32[256]{0:T(256)S(1)} %copy-done.6, s32[2048]{0:T(1024)S(1)} %add_select_fusion.9, s32[256]{0:T(256)S(1)} %copy-done.8), kind=kOutput, calls=%fused_computation.77 | convolution fusion | flops 550502400 | bytes 4466688 | tf_op jit(solution)/shard_map/dot_general | solution.py:26
  291.7 12.3 %multiply_convert_fusion = bf16[512,2048]{1,0:T(8,128)(2,1)} fusion(f32[512,2048]{1,0:T(8,128)S(1)} %fusion.44, bf16[512,256]{1,0:T(8,128)(2,1)S(1)} %copy-done.10, f32[2048]{0:T(1024)S(1)} %copy-done.12, s32[256]{0:T(256)S(1)} %copy-done.6, s32[2048]{0:T(1024)S(1)} %add_select_fusion.9, s32[256]{0:T(256)S(1)} %copy-done.8), kind=kOutput, calls=%fused_computation | convolution fusion | flops 553648128 | bytes 6572032 | tf_op jit(solution)/shard_map/dot_general | solution.py:26
  (54 shorter events, 2.9 us)
Async XLA Ops:
  6.5 2.8 copy-start
  6.5 101.9 %reduce-scatter.2.cloned.1.call-start = ((), (), s32[]{:S(2)}) async-start(), calls=%async_computation.3 | async-start | bytes 1310720 | tf_op jit(solution)/shard_map/reduce_scatter | solution.py:66
  8.6 13.2 %copy-start.5 = (s32[256]{0:T(256)}, s32[256]{0:T(256)S(1)}, u32[]{:S(2)}) copy-start(s32[256]{0:T(256)S(1)} %get-tuple-element.14) | copy-start | bytes 3076
  8.6 13.2 %copy-start.7 = (s32[256]{0:T(256)}, s32[256]{0:T(256)S(1)}, u32[]{:S(2)}) copy-start(s32[256]{0:T(256)S(1)} %get-tuple-element.15) | copy-start | bytes 3076
  9.3 12.6 %copy-start.11 = (f32[2048]{0:T(1024)S(1)}, f32[2048]{0:T(1024)}, u32[]{:S(2)}) copy-start(f32[2048]{0:T(1024)} %param.8) | copy-start | bytes 24580
  21.9 11.1 %copy-start.13 = (s32[8]{0:T(128)S(1)}, s32[8]{0:T(128)}, u32[]{:S(2)}) copy-start(s32[8]{0:T(128)} %param.10) | copy-start | bytes 100
  33.0 33.4 %copy-start.3 = (s32[512]{0:T(512)}, s32[512]{0:T(512)S(1)}, u32[]{:S(2)}) copy-start(s32[512]{0:T(512)S(1)} %add_select_fusion.16) | copy-start | bytes 6148
  33.2 10.7 %copy-start.14 = (bf16[256,512]{1,0:T(8,128)(2,1)S(1)}, bf16[256,512]{1,0:T(8,128)(2,1)}, u32[]{:S(2)}) copy-start(bf16[256,512]{1,0:T(8,128)(2,1)} %convolution_convert_fusion.3) | copy-start | bytes 786436
  78.3 74.6 %copy-start.1 = (bf16[256,256]{1,0:T(8,128)(2,1)S(1)}, bf16[256,256]{1,0:T(8,128)(2,1)}, u32[]{:S(2)}) copy-start(bf16[256,256]{1,0:T(8,128)(2,1)} %param.12) | copy-start | bytes 393220
  79.3 80.5 %copy-start.2 = (s32[8,16,16]{2,1,0:T(8,128)S(1)}, s32[8,16,16]{2,1,0:T(8,128)}, u32[]{:S(2)}) copy-start(s32[8,16,16]{2,1,0:T(8,128)} %param.13) | copy-start | bytes 24580
  79.3 73.6 %all-reduce.4.cloned.1.call-start = ((), (), s32[]{:S(2)}) async-start(), calls=%async_computation.4 | async-start | bytes 524288 | tf_op jit(solution)/shard_map/psum | solution.py:69
  155.5 15.1 %all-to-all-start = ((bf16[4,2,16384]{2,1,0:T(2,128)(2,1)}), bf16[4,2,16384]{2,1,0:T(2,128)(2,1)S(1)}, u32[]{:S(2)}, u32[]{:S(2)}) async-start(bf16[4,2,16384]{2,1,0:T(2,128)(2,1)} %reshape.290), calls=%async_computation.1 | async-start | bytes 524288 | tf_op jit(solution)/shard_map/all_to_all | solution.py:84
  159.9 55.4 %all-gather.2.cloned.1.call-start = ((), (), s32[]{:S(2)}) async-start(), calls=%async_computation.5 | async-start | bytes 1310720 | tf_op jit(solution)/shard_map/all_gather | solution.py:99
  173.9 41.3 %copy-start.4 = (s32[512]{0:T(512)S(1)}, s32[512]{0:T(512)}, u32[]{:S(2)}) copy-start(s32[512]{0:T(512)} %copy-done.3) | copy-start | bytes 6148
  186.3 93.5 %all-reduce.6.cloned.1.call-start = ((), (), s32[]{:S(2)}) async-start(), calls=%async_computation.6 | async-start | bytes 1048576 | tf_op jit(solution)/shard_map/psum | solution.py:110
  215.2 11.7 %copy-start.9 = (bf16[2,4,256,256]{3,2,1,0:T(8,128)(2,1)S(1)}, bf16[2,4,256,256]{3,2,1,0:T(8,128)(2,1)}, u32[]{:S(2)}) copy-start(bf16[2,4,256,256]{3,2,1,0:T(8,128)(2,1)} %all-gather.2.cloned.1.call-done) | copy-start | bytes 3145732
  249.2 30.5 %copy-start.6 = (s32[256]{0:T(256)S(1)}, s32[256]{0:T(256)}, u32[]{:S(2)}) copy-start(s32[256]{0:T(256)} %copy-done.5) | copy-start | bytes 3076
  249.2 30.5 %copy-start.8 = (s32[256]{0:T(256)S(1)}, s32[256]{0:T(256)}, u32[]{:S(2)}) copy-start(s32[256]{0:T(256)} %copy-done.7) | copy-start | bytes 3076
  279.7 12.0 %copy-start.10 = (bf16[512,256]{1,0:T(8,128)(2,1)S(1)}, bf16[512,256]{1,0:T(8,128)(2,1)}, u32[]{:S(2)}) copy-start(bf16[512,256]{1,0:T(8,128)(2,1)} %get-tuple-element.6) | copy-start | bytes 786436
  279.7 12.0 %copy-start.12 = (f32[2048]{0:T(1024)S(1)}, f32[2048]{0:T(1024)}, u32[]{:S(2)}) copy-start(f32[2048]{0:T(1024)} %param.8) | copy-start | bytes 24580
Sparse Core Ops, SparseCore 0:
  79.5 28.9 reduce-scatter.1
  111.4 41.4 all-reduce.3
  186.4 28.7 all-gather.1
  260.8 18.9 all-reduce.5
where the time goes:
time: 316 us; the launch traced here: 311 us
  matrix products  141 us (45%)
  waiting for transfers between devices  121 us (38%)
  local copies, waits for them, and re-layouts  17.5 us (6%)
  between operations  15 us (5%)
  blocking collectives  10.3 us (3%)
  starting transfers between devices  4.62 us (1%)
    dot_general x6, matrix products, product(): return jnp.dot(left, right, preferred_element_type=jnp.float32)  69.1 us
    psum x1, waiting for transfers between devices, body(): blocks = lax.psum(blocks, 'facet')  44.4 us
    reduce_scatter x1, waiting for transfers between devices, body(): lax.psum_scatter(terms.astype(jnp.bfloat16), 'band', scatter_dimension=2,...  29.1 us
    all_gather x1, waiting for transfers between devices, body(): piece = lax.all_gather(residual_grid, 'band', axis=2, tiled=True)  28.7 us
    psum x1, waiting for transfers between devices, body(): lax.psum(e_real.astype(jnp.bfloat16), 'sub').astype(jnp.float32)  19.1 us
    dot_general x1, matrix products, body(): jnp.einsum('xy,ky->xk', facets, col_imag, preferred_element_type=jnp.floa...  12.5 us
    dot_general x1, matrix products, body(): jnp.einsum('gkx,gkl->xl', back_imag, piece[0], preferred_element_type=jnp...  11.7 us
    dot_general x1, matrix products, body(): jnp.einsum('gkx,gkl->xl', back_real, piece[0], preferred_element_type=jnp...  11.4 us
  transfers between devices with their start and end apart: 5, of which 4 were waited for; matrix products, arithmetic and copies ran while one was open for 3% of the time, Pallas kernels for 0%

commit v1 on v0

v1 whole, which is shorter than its diff:
```python
import functools
import math

import jax
import jax.numpy as jnp
from jax import lax
from jax.experimental import pallas as pl
from jax.experimental.pallas import tpu as pltpu
from jax.sharding import PartitionSpec as P

IMAGE = 49152
QUARTER = IMAGE // 4
LANES = 128
FINE = 32
F32 = jnp.float32
BF16 = jnp.bfloat16
I32 = jnp.int32


def wrap(value):
    return value - float(IMAGE) * jnp.floor(value * (1.0 / IMAGE))


def phase_pair(first, second):
    upper = (first >> 8).astype(F32)
    lower = (first & 255).astype(F32)
    other = second.astype(F32)
    reduced = wrap(wrap(upper * other) * 256.0)
    reduced = wrap(reduced + lower * other)
    turn = jnp.floor(reduced * (1.0 / QUARTER) + 0.5)
    angle = (reduced - turn * float(QUARTER)) * (2.0 * math.pi / IMAGE)
    square = angle * angle
    sine = 1.0 / 120 + square * (-1.0 / 5040 + square * (1.0 / 362880))
    sine = angle + angle * square * (-1.0 / 6 + square * sine)
    cosine = -1.0 / 720 + square * (1.0 / 40320 + square * (-1.0 / 3628800))
    cosine = 1.0 + square * (-0.5 + square * (1.0 / 24 + square * cosine))
    quadrant = turn.astype(I32)
    odd = (quadrant & 1) == 1
    real = jnp.where(odd, sine, cosine)
    imag = jnp.where(odd, cosine, sine)
    real = jnp.where(((quadrant + 1) & 2) != 0, -real, real)
    imag = jnp.where((quadrant & 2) != 0, -imag, imag)
    return real, imag


def iota(shape, dim):
    return lax.broadcasted_iota(I32, shape, dim)


def nt(left, right):
    return lax.dot_general(left, right, (((1,), (1,)), ((), ())), preferred_element_type=F32)


def nn(left, right):
    return jnp.dot(left, right, preferred_element_type=F32)


def column_tables(column, offset, contrib, width, store):
    shape = (contrib, LANES)
    freq = column + iota(shape, 0)
    lane = iota(shape, 1)
    coarse_c, coarse_s = phase_pair(freq, offset + LANES * lane)
    fine_c, fine_s = phase_pair(freq, lane)
    for at in range(width // LANES):
        c = coarse_c[:, at : at + 1]
        s = coarse_s[:, at : at + 1]
        store(at, c * fine_c - s * fine_s, s * fine_c + c * fine_s)


def row_tables(start, offset, rows, contrib, store):
    coarse = rows // FINE
    cc, cs = phase_pair(
        start + iota((coarse, contrib), 1), offset + FINE * iota((coarse, contrib), 0)
    )
    fc, fs = phase_pair(start + iota((FINE, contrib), 1), iota((FINE, contrib), 0))
    for at in range(coarse):
        c = cc[at : at + 1, :]
        s = cs[at : at + 1, :]
        store(at * FINE, (c * fc - s * fs).astype(BF16), (s * fc + c * fs).astype(BF16))


def forward_kernel(offsets, starts, column, facets, window, out, cols, left, rows_tab):
    facet_at = lax.axis_index("facet")
    band_at = lax.axis_index("band")
    sub_at = lax.axis_index("sub")
    facet_count, band_count, piece, contrib = out.shape
    rows, width = facets.shape
    b_scale = 1.0 / math.sqrt(width)
    a_scale = 1.0 / math.sqrt(width * facet_count)

    def store_col(at, cosine, sine):
        here = slice(at * LANES, (at + 1) * LANES)
        taper = window[:, here]
        cols[0:contrib, here] = (cosine * taper).astype(BF16)
        cols[contrib:, here] = (sine * taper).astype(BF16)

    column_tables(column[0], offsets[facet_at, 1], contrib, width, store_col)
    t = nt(cols[...], facets[...]) * b_scale
    t_real = t[:contrib].astype(BF16)
    t_imag = (-t[contrib:]).astype(BF16)
    left[:contrib, :rows] = t_real
    left[:contrib, rows:] = t_imag
    left[contrib:, :rows] = t_imag
    left[contrib:, rows:] = -t_real
    position = offsets[facet_at, 0] + band_at * rows

    def step(g, carry):
        def store_row(at, cosine, sine):
            rows_tab[at : at + FINE, :] = cosine
            rows_tab[rows + at : rows + at + FINE, :] = sine

        row_tables(starts[sub_at * band_count + g], position, rows, contrib, store_row)
        part = nn(left[...], rows_tab[...]) * a_scale
        for f in range(facet_count):
            out[f, g] = part[f * piece : (f + 1) * piece].astype(BF16)
        return carry

    lax.fori_loop(0, band_count, step, 0)


def exchange_kernel(
    parts, kernel, kernel_t, counts, out,
    recv1, own2, recv2, planes,
    s1, r1, s2, r2, s3, r3, s4, r4, s5, r5, s6, r6,
):
    facet_at = lax.axis_index("facet")
    band_at = lax.axis_index("band")
    sub_at = lax.axis_index("sub")
    facet_count, band_count, piece, contrib = parts.shape
    sub_count = out.shape[0]
    half = facet_count // 2
    group = (facet_at // half) * half
    member = facet_at % half

    def remote(src, dst, send, recv, **where):
        return pltpu.make_async_remote_copy(
            src_ref=src, dst_ref=dst, send_sem=send, recv_sem=recv,
            device_id=where, device_id_type=pl.DeviceIdType.MESH,
        )

    barrier = pltpu.get_barrier_semaphore()
    for d in range(1, facet_count):
        pl.semaphore_signal(barrier, 1, device_id={"facet": lax.rem(facet_at + d, facet_count)},
                            device_id_type=pl.DeviceIdType.MESH)
    for d in range(1, band_count):
        pl.semaphore_signal(barrier, 1, device_id={"band": lax.rem(band_at + d, band_count)},
                            device_id_type=pl.DeviceIdType.MESH)
    for d in range(1, sub_count):
        pl.semaphore_signal(barrier, 1, device_id={"sub": lax.rem(sub_at + d, sub_count)},
                            device_id_type=pl.DeviceIdType.MESH)
    pl.semaphore_wait(barrier, facet_count + band_count + sub_count - 3)

    first = {}
    for e in range(band_count):
        g = lax.rem(band_at + 1 + e, band_count)
        for d in range(1, facet_count):
            peer = lax.rem(facet_at + d, facet_count)
            copy = remote(parts.at[peer, g], recv1.at[d - 1, g], s1.at[d - 1, e],
                          r1.at[d - 1, g], facet=peer)
            copy.start()
            first[d, e] = copy
    second = {}
    total = None
    for e in range(band_count):
        g = lax.rem(band_at + 1 + e, band_count)
        total = parts[facet_at, g].astype(F32)
        for d in range(1, facet_count):
            remote(parts.at[0, 0], recv1.at[d - 1, g], s1.at[d - 1, e], r1.at[d - 1, g],
                   facet=facet_at).wait_recv()
            total = total + recv1[d - 1, g].astype(F32)
        if e < band_count - 1:
            own2[e] = total.astype(BF16)
            copy = remote(own2.at[e], recv2.at[e], s2.at[e], r2.at[e], band=g)
            copy.start()
            second[e] = copy
    for e in range(band_count - 1):
        second[e].wait_recv()
        total = total + recv2[e].astype(F32)
    planes[member] = total.astype(BF16)
    third = {}
    for d in range(1, half):
        peer = group + lax.rem(member + d, half)
        copy = remote(planes.at[member], planes.at[member], s3.at[d - 1], r3.at[d - 1], facet=peer)
        copy.start()
        third[d] = copy
    tiles = counts.shape[1]
    side = contrib // tiles
    spread = (iota((contrib, tiles), 0) // side == iota((contrib, tiles), 1)).astype(BF16)
    mine = counts[sub_at * band_count + band_at].astype(F32).astype(BF16)
    seen = nt(nt(spread, mine).astype(BF16), spread)
    weight = seen / (seen + 4.0)
    for d in range(1, half):
        third[d].wait_recv()
    grid = planes[...].astype(F32).reshape(contrib, contrib).astype(BF16)
    y = nn(kernel[...], grid).astype(BF16)
    z = nt(y, kernel[...])
    w = (weight * z).astype(BF16)
    u = nn(w, kernel[...]).astype(BF16)
    first_row = pl.multiple_of(member * piece, piece)
    result = nn(kernel_t[pl.ds(first_row, piece), :], u)
    out[sub_at, band_at, facet_at] = result.astype(BF16)
    last = []

    def fan(b, f, to_facets):
        ref = out.at[sub_at, b, f]
        if to_facets:
            for d in range(1, facet_count):
                copy = remote(ref, ref, s5.at[d - 1, b], r5.at[d - 1, b],
                              facet=lax.rem(facet_at + d, facet_count))
                copy.start()
                last.append(copy)
        for d in range(1, sub_count):
            copy = remote(ref, ref, s6.at[d - 1, b, f], r6.at[d - 1, b, f],
                          sub=lax.rem(sub_at + d, sub_count))
            copy.start()
            last.append(copy)

    fourth = []
    for d in range(1, band_count):
        ref = out.at[sub_at, band_at, facet_at]
        copy = remote(ref, ref, s4.at[d - 1], r4.at[d - 1],
                      band=lax.rem(band_at + d, band_count))
        copy.start()
        fourth.append(copy)
    fan(band_at, facet_at, True)
    order = [d for pair in zip(range(1, band_count), range(band_count - 1, 0, -1)) for d in pair]
    order = list(dict.fromkeys(order))
    for d in order:
        b = lax.rem(band_at + band_count - d, band_count)
        ref = out.at[sub_at, b, facet_at]
        remote(ref, ref, s4.at[d - 1], r4.at[d - 1], band=b).wait_recv()
        fan(b, facet_at, True)
    for e in [0] + order:
        b = lax.rem(band_at + band_count - e, band_count)
        for d in range(1, facet_count):
            f = lax.rem(facet_at + facet_count - d, facet_count)
            ref = out.at[sub_at, b, f]
            remote(ref, ref, s5.at[d - 1, b], r5.at[d - 1, b], facet=f).wait_recv()
            fan(b, f, False)
    for d in range(1, sub_count):
        other = lax.rem(sub_at + d, sub_count)
        for b in range(band_count):
            for f in range(facet_count):
                ref = out.at[other, b, f]
                remote(ref, ref, s6.at[d - 1, b, f], r6.at[d - 1, b, f], sub=other).wait_recv()
    for copy in list(first.values()) + list(second.values()) + list(third.values()) + fourth + last:
        copy.wait_send()


def backward_kernel(offsets, starts, column, window, grids, out, cols, cos_tab, sin_tab, joined):
    facet_at = lax.axis_index("facet")
    band_at = lax.axis_index("band")
    sub_count, band_count, facet_count, piece, contrib = grids.shape
    rows, width = out.shape
    back_scale = 1.0 / math.sqrt(sub_count * band_count * contrib)
    out_scale = 1.0 / math.sqrt(contrib)
    position = offsets[facet_at, 0] + band_at * rows

    def step(s, carry):
        here = pl.ds(pl.multiple_of(s * contrib, contrib), contrib)

        def store_row(at, cosine, sine):
            cos_tab[at : at + FINE, here] = cosine
            sin_tab[at : at + FINE, here] = sine

        row_tables(starts[s], position, rows, contrib, store_row)
        block = grids[s // band_count, s % band_count].astype(F32)
        joined[:, here] = block.reshape(facet_count * piece, contrib).astype(BF16)
        return carry

    lax.fori_loop(0, sub_count * band_count, step, 0)

    def store_col(at, cosine, sine):
        here = slice(at * LANES, (at + 1) * LANES)
        cols[0:contrib, here] = cosine.astype(BF16)
        cols[contrib:, here] = sine.astype(BF16)

    column_tables(column[0], offsets[facet_at, 1], contrib, width, store_col)
    by_cos = nt(cos_tab[...], joined[...])
    by_sin = nt(sin_tab[...], joined[...])
    real = (by_cos[:, :contrib] - by_sin[:, contrib:]) * back_scale
    imag = (by_cos[:, contrib:] + by_sin[:, :contrib]) * back_scale
    both = jnp.concatenate([real.astype(BF16), (-imag).astype(BF16)], axis=1)
    step_width = min(width, 512)
    for at in range(width // step_width):
        here = slice(at * step_width, (at + 1) * step_width)
        image = nn(both, cols[:, here])
        out[:, here] = (window[:, here] * out_scale * image).astype(BF16)


def body(sizes, facets, window, facet_offsets, row_offsets, column_offset, kernel, tile_counts):
    facet_count, band_count, sub_count = sizes
    rows, width = facets.shape
    contrib = kernel.shape[0]
    subgrids = row_offsets.shape[0]
    piece = 2 * contrib // facet_count
    half = facet_count // 2
    smem = pl.BlockSpec(memory_space=pltpu.SMEM)
    vmem = pl.BlockSpec(memory_space=pltpu.VMEM)
    taper = window.reshape(1, width)
    parts = pl.pallas_call(
        forward_kernel,
        out_shape=jax.ShapeDtypeStruct((facet_count, band_count, piece, contrib), BF16),
        in_specs=[smem, smem, smem, vmem, vmem],
        out_specs=vmem,
        scratch_shapes=[
            pltpu.VMEM((2 * contrib, width), BF16),
            pltpu.VMEM((2 * contrib, 2 * rows), BF16),
            pltpu.VMEM((2 * rows, contrib), BF16),
        ],
        name="forward",
    )(facet_offsets, row_offsets, column_offset, facets, taper)
    dma = pltpu.SemaphoreType.DMA
    shapes = [
        (facet_count - 1, band_count),
        (band_count - 1,),
        (max(half - 1, 1),),
        (band_count - 1,),
        (facet_count - 1, band_count),
        (max(sub_count - 1, 1), band_count, facet_count),
    ]
    grids = pl.pallas_call(
        exchange_kernel,
        out_shape=jax.ShapeDtypeStruct((sub_count, band_count, facet_count, piece, contrib), BF16),
        in_specs=[vmem] * 4,
        out_specs=vmem,
        scratch_shapes=[
            pltpu.VMEM((facet_count - 1, band_count, piece, contrib), BF16),
            pltpu.VMEM((band_count - 1, piece, contrib), BF16),
            pltpu.VMEM((band_count - 1, piece, contrib), BF16),
            pltpu.VMEM((half, piece, contrib), BF16),
        ]
        + [dma(shape) for shape in shapes for _ in range(2)],
        compiler_params=pltpu.CompilerParams(collective_id=0, has_side_effects=True),
        name="exchange",
    )(parts, kernel, kernel.T, tile_counts)
    return pl.pallas_call(
        backward_kernel,
        out_shape=jax.ShapeDtypeStruct((rows, width), BF16),
        in_specs=[smem, smem, smem, vmem, vmem],
        out_specs=vmem,
        scratch_shapes=[
            pltpu.VMEM((2 * contrib, width), BF16),
            pltpu.VMEM((rows, subgrids * contrib), BF16),
            pltpu.VMEM((rows, subgrids * contrib), BF16),
            pltpu.VMEM((2 * contrib, subgrids * contrib), BF16),
        ],
        name="backward",
    )(facet_offsets, row_offsets, column_offset, taper, grids)


def solution(mesh):
    sizes = tuple(mesh.shape[axis] for axis in ("facet", "band", "sub"))
    in_specs = (P(("facet", "band"), None), P(), P(), P(), P(), P(), P())
    out_specs = P(("facet", "band"), None)
    return jax.shard_map(
        functools.partial(body, sizes), mesh=mesh, in_specs=in_specs, out_specs=out_specs, check_vma=False
    )
```

time: 316 us -> 61.1 us (0.19); the launches traced: 311 us -> 60.8 us
  matrix products: 141 us -> 0 us
  waiting for transfers between devices: 121 us -> 0 us
  Pallas kernels: 0 us -> 57.1 us
  local copies, waits for them, and re-layouts: 17.5 us -> 3.01 us
  between operations: 15 us -> 0.66 us
  blocking collectives: 10.3 us -> 0 us
  starting transfers between devices: 4.62 us -> 0 us
    dot_general x15 -> x0, matrix products: 141 us -> none  [the longest x6 69.1 us: product(): return jnp.dot(left, right, preferred_element_type=jnp.float32)]
    psum x2 -> x0, waiting for transfers between devices: 63.5 us -> none  [the longest x1 44.4 us: body(): blocks = lax.psum(blocks, 'facet')]
    pallas_call x0 -> x3, Pallas kernels: none -> 57.1 us  [the longest x1 41.1 us: body(): pl.pallas_call(exchange_kernel, out_shape=jax.ShapeDtypeStruct((sub_count...]
    reduce_scatter x1 -> x0, waiting for transfers between devices: 29.1 us -> none  [body(): lax.psum_scatter(terms.astype(jnp.bfloat16), 'band', scatter_dimension=2,...]
    all_gather x1 -> x0, waiting for transfers between devices: 28.7 us -> none  [body(): piece = lax.all_gather(residual_grid, 'band', axis=2, tiled=True)]
    all_to_all x1 -> x0, blocking collectives: 10.3 us -> none  [body(): lax.all_to_all(u_cols, 'band', split_axis=3, concat_axis=2, tiled=True)]
    reshape x1 -> x0, local copies, waits for them, and re-layouts: 6.09 us -> none  [body(): weights = weights.reshape(band_count, contrib, contrib)]
    all_to_all x1 -> x0, starting transfers between devices: 4.32 us -> none  [body(): lax.all_to_all(y_cols, 'band', split_axis=2, concat_axis=3, tiled=True)]
  transfers between devices with their start and end apart: 5 -> 0, of which waited for: 4 -> 0; matrix products, arithmetic and copies ran while one was open for 3% -> 0% of each run, Pallas kernels for 0% -> 0%
where the time goes in v1:
time: 61.1 us; the launch traced here: 60.8 us
  Pallas kernels  57.1 us (93%)
  local copies, waits for them, and re-layouts  3.01 us (5%)
  between operations  0.66 us (1%)
    pallas_call x1, Pallas kernels, body(): pl.pallas_call(exchange_kernel, out_shape=jax.ShapeDtypeStruct((sub_count...  41.1 us
    pallas_call x1, Pallas kernels, body(): pl.pallas_call(backward_kernel, out_shape=jax.ShapeDtypeStruct((rows, wid...  8.99 us
    pallas_call x1, Pallas kernels, body(): pl.pallas_call(forward_kernel, out_shape=jax.ShapeDtypeStruct((facet_coun...  7.02 us
    unnamed x2, local copies, waits for them, and re-layouts  3.01 us

profile of v1, /device:TPU:1, one launch (start us, length us, event | category | flops | bytes accessed | tf_op | source)
XLA Modules:
  0.0 60.8 jit_solution(5808597325779559508)
XLA Ops:
  0.7 1.4 %copy.10.offsets = s32[4,2]{1,0:T(4,128)} copy(s32[4,2]{0,1:T(2,128)} %param.9) | data formatting | bytes 64 | tf_op args[2]
  2.0 1.7 %copy.9 = bf16[256,256]{0,1:T(8,128)(2,1)} copy(bf16[256,256]{1,0:T(8,128)(2,1)} %kernel.1) | data formatting | bytes 262144 | tf_op args[5]
  3.7 7.0 %forward.1.parts = bf16[4,4,128,256]{3,2,1,0:T(8,128)(2,1)} custom-call(s32[4,2]{1,0:T(4,128)} %copy.10.offsets, s32[8]{0:T(128)} %starts.3, s32[1]{0:T(128)S(6)} %copy.11.column, bf16[512,2048]{1,0:T(8,128)(2,1)} %facets.1, f32[1,2048]{1,0:T(1,128)} %bitcast.3), custom_call_target="tpu_custom_call" | custom-call | tf_op jit(solution)/shard_map/forward/pallas_call | solution.py:301
  10.7 41.1 %exchange.1.grids = bf16[2,4,4,128,256]{4,3,2,1,0:T(8,128)(2,1)} custom-call(bf16[4,4,128,256]{3,2,1,0:T(8,128)(2,1)} %forward.1.parts, bf16[256,256]{1,0:T(8,128)(2,1)} %kernel.1, bf16[256,256]{1,0:T(8,128)(2,1)} %bitcast.2, s32[8,16,16]{2,1,0:T(8,128)} %counts.1), custom_call_target="tpu_custom_call" | custom-call | tf_op jit(solution)/shard_map/exchange/pallas_call | solution.py:322
  51.8 9.0 %backward.1 = bf16[512,2048]{1,0:T(8,128)(2,1)} custom-call(s32[4,2]{1,0:T(4,128)} %copy.10.offsets, s32[8]{0:T(128)} %starts.3, s32[1]{0:T(128)S(6)} %copy.11.column, f32[1,2048]{1,0:T(1,128)} %bitcast.4, bf16[2,4,4,128,256]{4,3,2,1,0:T(8,128)(2,1)} %exchange.1.grids), custom_call_target="tpu_custom_call" | custom-call | tf_op jit(solution)/shard_map/backward/pallas_call | solution.py:337

commit v2 on v1

v2 whole, which is shorter than its diff:
```python
import functools
import math

import jax
import jax.numpy as jnp
from jax import lax
from jax.experimental import pallas as pl
from jax.experimental.pallas import tpu as pltpu
from jax.sharding import PartitionSpec as P

IMAGE = 49152
QUARTER = IMAGE // 4
LANES = 128
FINE = 32
F32 = jnp.float32
BF16 = jnp.bfloat16
I32 = jnp.int32


def wrap(value):
    return value - float(IMAGE) * jnp.floor(value * (1.0 / IMAGE))


def phase_pair(first, second):
    upper = (first >> 8).astype(F32)
    lower = (first & 255).astype(F32)
    other = second.astype(F32)
    reduced = wrap(wrap(upper * other) * 256.0)
    reduced = wrap(reduced + lower * other)
    turn = jnp.floor(reduced * (1.0 / QUARTER) + 0.5)
    angle = (reduced - turn * float(QUARTER)) * (2.0 * math.pi / IMAGE)
    square = angle * angle
    sine = 1.0 / 120 + square * (-1.0 / 5040 + square * (1.0 / 362880))
    sine = angle + angle * square * (-1.0 / 6 + square * sine)
    cosine = -1.0 / 720 + square * (1.0 / 40320 + square * (-1.0 / 3628800))
    cosine = 1.0 + square * (-0.5 + square * (1.0 / 24 + square * cosine))
    quadrant = turn.astype(I32)
    odd = (quadrant & 1) == 1
    real = jnp.where(odd, sine, cosine)
    imag = jnp.where(odd, cosine, sine)
    real = jnp.where(((quadrant + 1) & 2) != 0, -real, real)
    imag = jnp.where((quadrant & 2) != 0, -imag, imag)
    return real, imag


def iota(shape, dim):
    return lax.broadcasted_iota(I32, shape, dim)


def nt(left, right):
    return lax.dot_general(left, right, (((1,), (1,)), ((), ())), preferred_element_type=F32)


def nn(left, right):
    return jnp.dot(left, right, preferred_element_type=F32)


def column_tables(column, offset, contrib, width, store):
    shape = (contrib, LANES)
    freq = column + iota(shape, 0)
    lane = iota(shape, 1)
    coarse_c, coarse_s = phase_pair(freq, offset + LANES * lane)
    fine_c, fine_s = phase_pair(freq, lane)
    for at in range(width // LANES):
        c = coarse_c[:, at : at + 1]
        s = coarse_s[:, at : at + 1]
        store(at, c * fine_c - s * fine_s, s * fine_c + c * fine_s)


def row_tables(start, offset, rows, contrib, store):
    coarse = rows // FINE
    cc, cs = phase_pair(
        start + iota((coarse, contrib), 1), offset + FINE * iota((coarse, contrib), 0)
    )
    fc, fs = phase_pair(start + iota((FINE, contrib), 1), iota((FINE, contrib), 0))
    for at in range(coarse):
        c = cc[at : at + 1, :]
        s = cs[at : at + 1, :]
        store(at * FINE, (c * fc - s * fs).astype(BF16), (s * fc + c * fs).astype(BF16))


def flat(block):
    pieces, rows, contrib = block.shape
    if rows % 16:
        return block.astype(F32).reshape(pieces * rows, contrib).astype(BF16)
    return block.reshape(pieces * rows, contrib)


def exchange_kernel(
    offsets, starts, column, facets_hbm, taper, kernel, counts,
    out, table_hbm,
    facets, cols, left, cos_tab, sin_tab, out_cols, kernel_t, parts,
    recv_a, recv_b, recv_c, recv_d, mid_a, mid_d, own2, recv2, planes, grids, by_cos, by_sin,
    load_sem, table_sem,
    sa, ra, sb, rb, sc, rc, sd, rd, s2, r2, s3, r3, s4, r4, slo, shi, r5, s6, r6,
):
    facet_at = lax.axis_index("facet")
    band_at = lax.axis_index("band")
    sub_at = lax.axis_index("sub")
    band_count, facet_count, piece, contrib = parts.shape
    sub_count = grids.shape[0]
    rows, width = facets.shape
    highs = facet_count // 2
    high = facet_at // 2
    low = facet_at % 2
    beside = high * 2 + (1 - low)
    group = (facet_at // highs) * highs
    member = facet_at % highs
    b_scale = 1.0 / math.sqrt(width)
    a_scale = 1.0 / math.sqrt(width * facet_count)
    back_scale = 1.0 / math.sqrt(sub_count * band_count * contrib)
    started = []

    def remote(src, dst, send, recv, **where):
        return pltpu.make_async_remote_copy(
            src_ref=src, dst_ref=dst, send_sem=send, recv_sem=recv,
            device_id=where, device_id_type=pl.DeviceIdType.MESH,
        )

    def send(*args, **where):
        copy = remote(*args, **where)
        copy.start()
        started.append(copy)

    def across(d):
        return lax.rem(high + d, highs)

    load = pltpu.make_async_copy(facets_hbm, facets, load_sem)
    load.start()
    barrier = pltpu.get_barrier_semaphore()
    for axis, at, count in (
        ("facet", facet_at, facet_count), ("band", band_at, band_count), ("sub", sub_at, sub_count)
    ):
        for d in range(1, count):
            pl.semaphore_signal(barrier, 1, device_id={axis: lax.rem(at + d, count)},
                                device_id_type=pl.DeviceIdType.MESH)

    def store_taper(at, cosine, sine):
        here = slice(at * LANES, (at + 1) * LANES)
        cols[0:contrib, here] = (cosine * taper[:, here]).astype(BF16)
        cols[contrib:, here] = (sine * taper[:, here]).astype(BF16)

    def store_plain(at, cosine, sine):
        here = slice(at * LANES, (at + 1) * LANES)
        out_cols[0:contrib, here] = cosine.astype(BF16)
        out_cols[contrib:, here] = sine.astype(BF16)

    offset_y = offsets[1, facet_at]
    position = offsets[0, facet_at] + band_at * rows

    def make_rows(s):
        def store_row(at, cosine, sine):
            cos_tab[s, at : at + FINE, :] = cosine
            sin_tab[s, at : at + FINE, :] = sine

        row_tables(starts[s], position, rows, contrib, store_row)

    column_tables(column[0], offset_y, contrib, width, store_taper)
    load.wait()
    t = nt(cols[...], facets[...]) * b_scale
    t_real = t[:contrib].astype(BF16)
    t_imag = (-t[contrib:]).astype(BF16)
    left[:contrib, :rows] = t_real
    left[:contrib, rows:] = t_imag
    left[contrib:, :rows] = t_imag
    left[contrib:, rows:] = -t_real

    def owner(e):
        return lax.rem(band_at + 1 + e, band_count)

    for e in range(band_count):
        g = owner(e)
        s = sub_at * band_count + g
        make_rows(s)
        part = (nn(left[:, :rows], cos_tab[s]) + nn(left[:, rows:], sin_tab[s])) * a_scale
        for f in range(facet_count):
            parts[g, f] = part[f * piece : (f + 1) * piece].astype(BF16)
        if e == 0:
            pl.semaphore_wait(barrier, facet_count + band_count + sub_count - 3)
        if e % 2 == 0:
            for h in range(highs):
                send(parts.at[g, 2 * h + 1 - low], recv_a.at[e, h], sa.at[e, h], ra.at[e, h],
                     facet=beside)
        else:
            for d in range(1, highs):
                send(parts.at[g, pl.ds(2 * across(d), 2)], recv_c.at[e, d - 1], sc.at[e, d - 1],
                     rc.at[e, d - 1], facet=2 * across(d) + low)
    for d in range(1, sub_count):
        def other_rows(b, carry, d=d):
            make_rows(lax.rem(sub_at + d, sub_count) * band_count + b)
            return carry

        lax.fori_loop(0, band_count, other_rows, 0)

    def second_hop(e):
        g = owner(e)
        if e % 2 == 0:
            for h in range(highs):
                remote(parts.at[g, 0], recv_a.at[e, h], sa.at[e, h], ra.at[e, h],
                       facet=beside).wait_recv()
            for d in range(1, highs):
                h = across(d)
                mine = parts[g, 2 * h + low].astype(F32) + recv_a[e, h].astype(F32)
                mid_a[e, d - 1] = mine.astype(BF16)
                send(mid_a.at[e, d - 1], recv_b.at[e, d - 1], sb.at[e, d - 1], rb.at[e, d - 1],
                     facet=2 * h + low)
        else:
            mine = parts[g, beside].astype(F32)
            for d in range(1, highs):
                remote(parts.at[g, pl.ds(0, 2)], recv_c.at[e, d - 1], sc.at[e, d - 1],
                       rc.at[e, d - 1], facet=beside).wait_recv()
                mine = mine + recv_c[e, d - 1, 1 - low].astype(F32)
            mid_d[e] = mine.astype(BF16)
            send(mid_d.at[e], recv_d.at[e], sd.at[e], rd.at[e], facet=beside)

    def facet_sum(e):
        g = owner(e)
        total = parts[g, facet_at].astype(F32)
        if e % 2 == 0:
            total = total + recv_a[e, high].astype(F32)
            for d in range(1, highs):
                remote(mid_a.at[e, d - 1], recv_b.at[e, d - 1], sb.at[e, d - 1], rb.at[e, d - 1],
                       facet=beside).wait_recv()
                total = total + recv_b[e, d - 1].astype(F32)
        else:
            for d in range(1, highs):
                total = total + recv_c[e, d - 1, low].astype(F32)
            remote(mid_d.at[e], recv_d.at[e], sd.at[e], rd.at[e], facet=beside).wait_recv()
            total = total + recv_d[e].astype(F32)
        if e < band_count - 1:
            own2[e] = total.astype(BF16)
            send(own2.at[e], recv2.at[e], s2.at[e], r2.at[e], band=g)
        return total

    second_hop(0)
    for e in range(1, band_count):
        second_hop(e)
        facet_sum(e - 1)
    kernel_t[...] = kernel[...].T
    tiles = counts.shape[1]
    side = contrib // tiles
    spread = (iota((contrib, tiles), 0) // side == iota((contrib, tiles), 1)).astype(BF16)
    tile = counts[sub_at * band_count + band_at].astype(F32).astype(BF16)
    seen = nt(nt(spread, tile).astype(BF16), spread)
    weight = seen / (seen + 4.0)
    total = facet_sum(band_count - 1)
    for e in range(band_count - 1):
        remote(own2.at[e], recv2.at[e], s2.at[e], r2.at[e], band=band_at).wait_recv()
        total = total + recv2[e].astype(F32)
    planes[member] = total.astype(BF16)
    for d in range(1, highs):
        send(planes.at[member], planes.at[member], s3.at[d - 1], r3.at[d - 1],
             facet=group + lax.rem(member + d, highs))
    for d in range(1, highs):
        there = lax.rem(member + highs - d, highs)
        remote(planes.at[there], planes.at[there], s3.at[d - 1], r3.at[d - 1],
               facet=beside).wait_recv()
    y = nn(kernel[...], flat(planes[...])).astype(BF16)
    z = nt(y, kernel[...])
    w = (weight * z).astype(BF16)
    u = nn(w, kernel[...]).astype(BF16)
    first_row = pl.multiple_of(member * piece, piece)
    result = nn(kernel_t[pl.ds(first_row, piece), :], u)
    grids[sub_at, band_at, facet_at] = result.astype(BF16)

    def origin(e):
        return lax.rem(band_at + band_count - e, band_count)

    def to_core(b, f):
        ref = grids.at[sub_at, b, f]
        for d in range(1, sub_count):
            send(ref, ref, s6.at[d - 1, b, f], r6.at[d - 1, b, f],
                 sub=lax.rem(sub_at + d, sub_count))

    def to_beside(b, f):
        ref = grids.at[sub_at, b, f]
        send(ref, ref, slo.at[b, f], r5.at[b, f], facet=beside)

    def to_highs(b, f, slot):
        ref = grids.at[sub_at, b, f]
        for d in range(1, highs):
            send(ref, ref, shi.at[slot, b, d - 1], r5.at[b, f], facet=2 * across(d) + low)

    def arrived(b, f):
        ref = grids.at[sub_at, b, f]
        remote(ref, ref, slo.at[b, f], r5.at[b, f], facet=beside).wait_recv()

    def fan(e):
        b = origin(e)
        if e > 0:
            ref = grids.at[sub_at, b, facet_at]
            remote(ref, ref, s4.at[e - 1], r4.at[e - 1], band=b).wait_recv()
        to_beside(b, facet_at)
        to_highs(b, facet_at, 0)
        to_core(b, facet_at)

    def forward(e):
        b = origin(e)
        arrived(b, beside)
        if e % 2 == 0:
            to_highs(b, beside, 1)
        to_core(b, beside)
        for d in range(1, highs):
            f = 2 * across(d) + low
            arrived(b, f)
            if e % 2 == 1:
                to_beside(b, f)
            to_core(b, f)

    def finish(e):
        b = origin(e)
        for d in range(1, highs):
            f = 2 * across(d) + 1 - low
            arrived(b, f)
            to_core(b, f)

    for d in range(1, band_count):
        ref = grids.at[sub_at, band_at, facet_at]
        send(ref, ref, s4.at[d - 1], r4.at[d - 1], band=lax.rem(band_at + d, band_count))

    def gather(sub, b, fresh):
        s = sub * band_count + b
        block = flat(grids[sub, b])
        if fresh:
            by_cos[...] = nt(cos_tab[s], block)
            by_sin[...] = nt(sin_tab[s], block)
        else:
            by_cos[...] += nt(cos_tab[s], block)
            by_sin[...] += nt(sin_tab[s], block)

    def gather_other(e):
        b = origin(e)
        for d in range(1, sub_count):
            other = lax.rem(sub_at + d, sub_count)
            for f in range(facet_count):
                ref = grids.at[other, b, f]
                remote(ref, ref, s6.at[d - 1, b, f], r6.at[d - 1, b, f], sub=other).wait_recv()
            gather(other, b, False)

    order = [d for pair in zip(range(1, band_count), range(band_count - 1, 0, -1)) for d in pair]
    order = [0] + list(dict.fromkeys(order))
    fan(order[0])
    column_tables(column[0], offset_y, contrib, width, store_plain)
    table = pltpu.make_async_copy(out_cols, table_hbm, table_sem)
    table.start()
    for before, e in zip(order, order[1:]):
        fan(e)
        forward(before)
    forward(order[-1])
    finish(order[0])
    gather(sub_at, origin(order[0]), True)
    for before, e in zip(order, order[1:]):
        finish(e)
        gather_other(before)
        gather(sub_at, origin(e), False)
    gather_other(order[-1])
    real = (by_cos[:, :contrib] - by_sin[:, contrib:]) * back_scale
    imag = (by_cos[:, contrib:] + by_sin[:, :contrib]) * back_scale
    out[:, :contrib] = real.astype(BF16)
    out[:, contrib:] = (-imag).astype(BF16)
    table.wait()
    for copy in started:
        copy.wait_send()


def image_kernel(both, table, taper, out):
    scale = 1.0 / math.sqrt(both.shape[1] // 2)
    out[...] = (taper[...] * scale * nn(both[...], table[...])).astype(BF16)


def body(sizes, facets, window, facet_offsets, row_offsets, column_offset, kernel, tile_counts):
    facet_count, band_count, sub_count = sizes
    rows, width = facets.shape
    contrib = kernel.shape[0]
    subgrids = row_offsets.shape[0]
    piece = 2 * contrib // facet_count
    highs = facet_count // 2
    more = max(highs - 1, 1)
    smem = pl.BlockSpec(memory_space=pltpu.SMEM)
    vmem = pl.BlockSpec(memory_space=pltpu.VMEM)
    anywhere = pl.BlockSpec(memory_space=pl.ANY)
    taper = window.reshape(1, width)
    dma = pltpu.SemaphoreType.DMA

    def buffer(*shape, dtype=BF16):
        return pltpu.VMEM(shape, dtype)

    both, table = pl.pallas_call(
        exchange_kernel,
        out_shape=(
            jax.ShapeDtypeStruct((rows, 2 * contrib), BF16),
            jax.ShapeDtypeStruct((2 * contrib, width), BF16),
        ),
        in_specs=[smem, smem, smem, anywhere, vmem, vmem, vmem],
        out_specs=(vmem, anywhere),
        scratch_shapes=[
            buffer(rows, width),
            buffer(2 * contrib, width),
            buffer(2 * contrib, 2 * rows),
            buffer(subgrids, rows, contrib),
            buffer(subgrids, rows, contrib),
            buffer(2 * contrib, width),
            buffer(contrib, contrib),
            buffer(band_count, facet_count, piece, contrib),
            buffer(band_count, highs, piece, contrib),
            buffer(band_count, more, piece, contrib),
            buffer(band_count, more, 2, piece, contrib),
            buffer(band_count, piece, contrib),
            buffer(band_count, more, piece, contrib),
            buffer(band_count, piece, contrib),
            buffer(band_count - 1, piece, contrib),
            buffer(band_count - 1, piece, contrib),
            buffer(highs, piece, contrib),
            buffer(sub_count, band_count, facet_count, piece, contrib),
            buffer(rows, 2 * contrib, dtype=F32),
            buffer(rows, 2 * contrib, dtype=F32),
            dma,
            dma,
        ]
        + [dma((band_count, highs))] * 2
        + [dma((band_count, more))] * 4
        + [dma((band_count,))] * 2
        + [dma((band_count - 1,))] * 2
        + [dma((more,))] * 2
        + [dma((band_count - 1,))] * 2
        + [
            dma((band_count, facet_count)),
            dma((2, band_count, more)),
            dma((band_count, facet_count)),
        ]
        + [dma((max(sub_count - 1, 1), band_count, facet_count))] * 2,
        compiler_params=pltpu.CompilerParams(collective_id=0, has_side_effects=True),
        name="exchange",
    )(facet_offsets.T, row_offsets, column_offset, facets, taper, kernel, tile_counts)
    wide = min(width, 512)
    return pl.pallas_call(
        image_kernel,
        grid=(width // wide,),
        out_shape=jax.ShapeDtypeStruct((rows, width), BF16),
        in_specs=[
            pl.BlockSpec((rows, 2 * contrib), lambda i: (0, 0)),
            pl.BlockSpec((2 * contrib, wide), lambda i: (0, i)),
            pl.BlockSpec((1, wide), lambda i: (0, i)),
        ],
        out_specs=pl.BlockSpec((rows, wide), lambda i: (0, i)),
        name="image",
    )(both, table, taper)


def solution(mesh):
    sizes = tuple(mesh.shape[axis] for axis in ("facet", "band", "sub"))
    in_specs = (P(("facet", "band"), None), P(), P(), P(), P(), P(), P())
    out_specs = P(("facet", "band"), None)
    return jax.shard_map(
        functools.partial(body, sizes), mesh=mesh, in_specs=in_specs, out_specs=out_specs, check_vma=False
    )
```

time: 61.1 us -> 53 us (0.87)
  Pallas kernels: 57.1 us -> 52.1 us
  local copies, waits for them, and re-layouts: 3.01 us -> 0 us
    pallas_call x3 -> x2, Pallas kernels: 57.1 us -> 52.1 us  [the longest x1 47.2 us: body(): pl.pallas_call(exchange_kernel, out_shape=(jax.ShapeDtypeStruct((rows, 2...]
    unnamed x2 -> x0, local copies, waits for them, and re-layouts: 3.01 us -> none
where the time goes in v2:
time: 53 us; the launch traced here: 52.8 us
  Pallas kernels  52.1 us (98%)
  between operations  0.66 us (1%)
    pallas_call x1, Pallas kernels, body(): pl.pallas_call(exchange_kernel, out_shape=(jax.ShapeDtypeStruct((rows, 2...  47.2 us
    pallas_call x1, Pallas kernels, body(): pl.pallas_call(image_kernel, grid=(width // wide,), out_shape=jax.ShapeDt...  4.95 us

profile of v2, /device:TPU:1, one launch (start us, length us, event | category | flops | bytes accessed | tf_op | source)
XLA Modules:
  0.0 52.8 jit_solution(17777603873770988301)
XLA Ops:
  0.7 47.2 %exchange.1 = (bf16[512,512]{1,0:T(8,128)(2,1)}, bf16[512,2048]{1,0:T(8,128)(2,1)}) custom-call(s32[2,4]{1,0:T(2,128)} %bitcast.4, s32[8]{0:T(128)} %starts.1, s32[1]{0:T(128)S(6)} %copy.8.column, bf16[512,2048]{1,0:T(8,128)(2,1)} %facets_hbm.1, f32[1,2048]{1,0:T(1,128)} %bitcast.2, bf16[256,256]{1,0:T(8,128)(2,1)} %kernel.1, s32[8,16,16]{2,1,0:T(8,128)} %counts.1), custom_call_target="tpu_custom_call" | custom-call | tf_op jit(solution)/shard_map/exchange/pallas_call | solution.py:388
  47.8 5.0 %image.1 = bf16[512,2048]{1,0:T(8,128)(2,1)} custom-call(bf16[512,512]{1,0:T(8,128)(2,1)} %get-tuple-element.7.both, bf16[512,2048]{1,0:T(8,128)(2,1)} %get-tuple-element.8.table, f32[1,2048]{1,0:T(1,128)} %bitcast.3), custom_call_target="tpu_custom_call" | custom-call | tf_op jit(solution)/shard_map/image/pallas_call | solution.py:436

commit v3 on v2

--- a/solution.py
+++ b/solution.py
@@ -88,10 +88,10 @@
 
 def exchange_kernel(
     offsets, starts, column, facets_hbm, taper, kernel, counts,
-    out, table_hbm,
-    facets, cols, left, cos_tab, sin_tab, out_cols, kernel_t, parts,
+    out, out_cols,
+    facets, cols, left, cos_tab, sin_tab, kernel_t, parts,
     recv_a, recv_b, recv_c, recv_d, mid_a, mid_d, own2, recv2, planes, grids, by_cos, by_sin,
-    load_sem, table_sem,
+    load_sem,
     sa, ra, sb, rb, sc, rc, sd, rd, s2, r2, s3, r3, s4, r4, slo, shi, r5, s6, r6,
 ):
     facet_at = lax.axis_index("facet")
@@ -341,8 +341,6 @@
     order = [0] + list(dict.fromkeys(order))
     fan(order[0])
     column_tables(column[0], offset_y, contrib, width, store_plain)
-    table = pltpu.make_async_copy(out_cols, table_hbm, table_sem)
-    table.start()
     for before, e in zip(order, order[1:]):
         fan(e)
         forward(before)
@@ -358,14 +356,15 @@
     imag = (by_cos[:, contrib:] + by_sin[:, :contrib]) * back_scale
     out[:, :contrib] = real.astype(BF16)
     out[:, contrib:] = (-imag).astype(BF16)
-    table.wait()
     for copy in started:
         copy.wait_send()
 
 
 def image_kernel(both, table, taper, out):
     scale = 1.0 / math.sqrt(both.shape[1] // 2)
-    out[...] = (taper[...] * scale * nn(both[...], table[...])).astype(BF16)
+    wide = out.shape[1]
+    here = pl.ds(pl.multiple_of(pl.program_id(0) * wide, wide), wide)
+    out[...] = (taper[:, here] * scale * nn(both[...], table[:, here])).astype(BF16)
 
 
 def body(sizes, facets, window, facet_offsets, row_offsets, column_offset, kernel, tile_counts):
@@ -388,18 +387,17 @@
     both, table = pl.pallas_call(
         exchange_kernel,
         out_shape=(
-            jax.ShapeDtypeStruct((rows, 2 * contrib), BF16),
-            jax.ShapeDtypeStruct((2 * contrib, width), BF16),
+            pltpu.VMEM((rows, 2 * contrib), BF16),
+            pltpu.VMEM((2 * contrib, width), BF16),
         ),
         in_specs=[smem, smem, smem, anywhere, vmem, vmem, vmem],
-        out_specs=(vmem, anywhere),
+        out_specs=(vmem, vmem),
         scratch_shapes=[
             buffer(rows, width),
             buffer(2 * contrib, width),
             buffer(2 * contrib, 2 * rows),
             buffer(subgrids, rows, contrib),
             buffer(subgrids, rows, contrib),
-            buffer(2 * contrib, width),
             buffer(contrib, contrib),
             buffer(band_count, facet_count, piece, contrib),
             buffer(band_count, highs, piece, contrib),
@@ -415,7 +413,6 @@
             buffer(rows, 2 * contrib, dtype=F32),
             buffer(rows, 2 * contrib, dtype=F32),
             dma,
-            dma,
         ]
         + [dma((band_count, highs))] * 2
         + [dma((band_count, more))] * 4
@@ -429,20 +426,21 @@
             dma((band_count, facet_count)),
         ]
         + [dma((max(sub_count - 1, 1), band_count, facet_count))] * 2,
-        compiler_params=pltpu.CompilerParams(collective_id=0, has_side_effects=True),
+        compiler_params=pltpu.CompilerParams(
+            collective_id=0, has_side_effects=True
+        ),
         name="exchange",
     )(facet_offsets.T, row_offsets, column_offset, facets, taper, kernel, tile_counts)
     wide = min(width, 512)
+    both = pltpu.with_memory_space_constraint(both, pltpu.VMEM)
+    table = pltpu.with_memory_space_constraint(table, pltpu.VMEM)
     return pl.pallas_call(
         image_kernel,
         grid=(width // wide,),
         out_shape=jax.ShapeDtypeStruct((rows, width), BF16),
-        in_specs=[
-            pl.BlockSpec((rows, 2 * contrib), lambda i: (0, 0)),
-            pl.BlockSpec((2 * contrib, wide), lambda i: (0, i)),
-            pl.BlockSpec((1, wide), lambda i: (0, i)),
-        ],
+        in_specs=[vmem, vmem, vmem],
         out_specs=pl.BlockSpec((rows, wide), lambda i: (0, i)),
+        compiler_params=pltpu.CompilerParams(vmem_limit_bytes=16 << 20),
         name="image",
     )(both, table, taper)
 

time: 53 us -> 50.2 us (0.947)
  Pallas kernels: 52.1 us -> 49.3 us
    pallas_call x1, Pallas kernels: 4.95 us -> 2.94 us  [body(): pl.pallas_call(image_kernel, grid=(width // wide,), out_shape=jax.ShapeDt...]
    pallas_call x1, Pallas kernels: 47.2 us -> 46.4 us  [body(): pl.pallas_call(exchange_kernel, out_shape=(pltpu.VMEM((rows, 2 * contrib)...]
where the time goes in v3:
time: 50.2 us; the launch traced here: 50 us
  Pallas kernels  49.3 us (98%)
  between operations  0.68 us (1%)
    pallas_call x1, Pallas kernels, body(): pl.pallas_call(exchange_kernel, out_shape=(pltpu.VMEM((rows, 2 * contrib)...  46.4 us
    pallas_call x1, Pallas kernels, body(): pl.pallas_call(image_kernel, grid=(width // wide,), out_shape=jax.ShapeDt...  2.94 us

profile of v3, /device:TPU:1, one launch (start us, length us, event | category | flops | bytes accessed | tf_op | source)
XLA Modules:
  0.0 50.0 jit_solution(528523828304585133)
XLA Ops:
  0.0 0.0 copy-start
  0.7 46.4 %exchange.1 = (bf16[512,512]{1,0:T(8,128)(2,1)S(1)}, bf16[512,2048]{1,0:T(8,128)(2,1)S(1)}) custom-call(s32[2,4]{1,0:T(2,128)} %bitcast.4, s32[8]{0:T(128)} %starts.1, s32[1]{0:T(128)S(6)} %copy.8.column, bf16[512,2048]{1,0:T(8,128)(2,1)} %facets_hbm.1, f32[1,2048]{1,0:T(1,128)} %bitcast.2, bf16[256,256]{1,0:T(8,128)(2,1)} %kernel.1, s32[8,16,16]{2,1,0:T(8,128)} %counts.1), custom_call_target="tpu_custom_call" | custom-call | tf_op jit(solution)/shard_map/exchange/pallas_call | solution.py:387
  47.1 0.0 copy-done
  47.1 2.9 %image.1 = bf16[512,2048]{1,0:T(8,128)(2,1)} custom-call(bf16[512,512]{1,0:T(8,128)(2,1)S(1)} %get-tuple-element.7.both, bf16[512,2048]{1,0:T(8,128)(2,1)S(1)} %get-tuple-element.8.table, f32[1,2048]{1,0:T(1,128)S(1)} %bitcast.3), custom_call_target="tpu_custom_call" | custom-call | tf_op jit(solution)/shard_map/image/pallas_call | solution.py:437
Async XLA Ops:
  0.0 47.1 %copy-start = (f32[2048]{0:T(1024)S(1)}, f32[2048]{0:T(1024)}, u32[]{:S(2)}) copy-start(f32[2048]{0:T(1024)} %param.8) | copy-start | bytes 24580

commit v4 on v3

--- a/solution.py
+++ b/solution.py
@@ -165,8 +165,10 @@
     left[contrib:, :rows] = t_imag
     left[contrib:, rows:] = -t_real
 
+    shifts = sorted(range(1, band_count), key=lambda d: abs(2 * d - band_count)) + [0]
+
     def owner(e):
-        return lax.rem(band_at + 1 + e, band_count)
+        return lax.rem(band_at + shifts[e], band_count)
 
     for e in range(band_count):
         g = owner(e)
@@ -191,6 +193,7 @@
             return carry
 
         lax.fori_loop(0, band_count, other_rows, 0)
+    column_tables(column[0], offset_y, contrib, width, store_plain)
 
     def second_hop(e):
         g = owner(e)
@@ -340,17 +343,18 @@
     order = [d for pair in zip(range(1, band_count), range(band_count - 1, 0, -1)) for d in pair]
     order = [0] + list(dict.fromkeys(order))
     fan(order[0])
-    column_tables(column[0], offset_y, contrib, width, store_plain)
     for before, e in zip(order, order[1:]):
         fan(e)
         forward(before)
-    forward(order[-1])
     finish(order[0])
     gather(sub_at, origin(order[0]), True)
+    forward(order[-1])
     for before, e in zip(order, order[1:]):
+        if e != order[1]:
+            gather(sub_at, origin(before), False)
         finish(e)
         gather_other(before)
-        gather(sub_at, origin(e), False)
+    gather(sub_at, origin(order[-1]), False)
     gather_other(order[-1])
     real = (by_cos[:, :contrib] - by_sin[:, contrib:]) * back_scale
     imag = (by_cos[:, contrib:] + by_sin[:, :contrib]) * back_scale

time: 50.2 us -> 49.5 us (0.986)
  Pallas kernels: 49.3 us -> 48.7 us
    pallas_call x1, Pallas kernels: 46.4 us -> 45.7 us  [body(): pl.pallas_call(exchange_kernel, out_shape=(pltpu.VMEM((rows, 2 * contrib)...]
where the time goes in v4:
time: 49.5 us; the launch traced here: 49.4 us
  Pallas kernels  48.7 us (98%)
  between operations  0.68 us (1%)
    pallas_call x1, Pallas kernels, body(): pl.pallas_call(exchange_kernel, out_shape=(pltpu.VMEM((rows, 2 * contrib)...  45.7 us
    pallas_call x1, Pallas kernels, body(): pl.pallas_call(image_kernel, grid=(width // wide,), out_shape=jax.ShapeDt...  2.94 us

profile of v4, /device:TPU:1, one launch (start us, length us, event | category | flops | bytes accessed | tf_op | source)
XLA Modules:
  0.0 49.4 jit_solution(15169693558519458162)
XLA Ops:
  0.0 0.0 copy-start
  0.7 45.7 %exchange.1 = (bf16[512,512]{1,0:T(8,128)(2,1)S(1)}, bf16[512,2048]{1,0:T(8,128)(2,1)S(1)}) custom-call(s32[2,4]{1,0:T(2,128)} %bitcast.4, s32[8]{0:T(128)} %starts.1, s32[1]{0:T(128)S(6)} %copy.8.column, bf16[512,2048]{1,0:T(8,128)(2,1)} %facets_hbm.1, f32[1,2048]{1,0:T(1,128)} %bitcast.2, bf16[256,256]{1,0:T(8,128)(2,1)} %kernel.1, s32[8,16,16]{2,1,0:T(8,128)} %counts.1), custom_call_target="tpu_custom_call" | custom-call | tf_op jit(solution)/shard_map/exchange/pallas_call | solution.py:391
  46.4 0.0 copy-done
  46.4 2.9 %image.1 = bf16[512,2048]{1,0:T(8,128)(2,1)} custom-call(bf16[512,512]{1,0:T(8,128)(2,1)S(1)} %get-tuple-element.7.both, bf16[512,2048]{1,0:T(8,128)(2,1)S(1)} %get-tuple-element.8.table, f32[1,2048]{1,0:T(1,128)S(1)} %bitcast.3), custom_call_target="tpu_custom_call" | custom-call | tf_op jit(solution)/shard_map/image/pallas_call | solution.py:441
Async XLA Ops:
  0.0 46.4 %copy-start = (f32[2048]{0:T(1024)S(1)}, f32[2048]{0:T(1024)}, u32[]{:S(2)}) copy-start(f32[2048]{0:T(1024)} %param.8) | copy-start | bytes 24580
